TPU v7x, 32 devices: a whole 2x2x4 slice. The times are simulated.
32 devices in a mesh: pix: 8 (over z, y), ang: 4 (over x, core).
Axes of the slice: x: 2, y: 2, z: 4, core: 2. Of those that a mesh axis runs over, the one named last changes fastest.
Arguments:
- tiles: float32 [8, 4, 512, 4096], P('pix', 'ang'), may hold values from 0.01 to 1
- tile_ray: int32 [8, 4, 512], P('pix', 'ang'), may hold values from 0 to 31, as said below
- tile_pix: int32 [8, 4, 512], P('pix', 'ang'), may hold values from 0 to 7, as said below
- tile_count: int32 [8, 4], P('pix', 'ang'), may hold values from 128 to 512, as said below
- ray_slot: int32 [4, 32], P('ang'), may hold values from 0 to 31, as said below
- image: float32 [4096, 128], P(('pix', 'ang')), may hold values from 0 to 2
- measured: float32 [4, 2048, 128], P('ang', 'pix'), may hold values from -6144 to 6144
Outputs:
- new_image: float32 [4096, 128], P(('pix', 'ang'))
- scaled_resid: float32 [4, 2048, 128], P('ang', 'pix')
Inputs may be any that keep to these rules, and one draw needn't show every extreme that they name: Device (p, a) uses only its first tile_count[p, a] tiles; some device uses all 512. `tile_ray`: the used tiles of the devices of one angle group a together name every ray block of that group. `tile_pix`: the used tiles of the devices of one region p together name every pixel block of that region. `ray_slot`: each row is a permutation; slot s lies on the device with pix index s // 4.
All inputs are finite; a program needn't handle non-finite values.
Results may differ from a plain program's by a relative error of at most 0.0003.
Values sent between devices are 32-bit elements; how exact they have to be, the bound alone decides.
No kernel may reach another device: no remote copies, remote signals or barrier semaphores. Data moves between devices by JAX's collectives and lax.ppermute only.
A program may use at most 64 MiB of HBM per device.

v0:
```python
import functools

import jax
import jax.numpy as jnp
import numpy as np
from jax import lax
from jax.experimental import pallas as pl
from jax.experimental.pallas import tpu as pltpu
from jax.sharding import PartitionSpec as P


RELAX = 0.9
F32 = jnp.float32
BF16 = jnp.bfloat16
EXTRA = 8


def split(x):
    high = x.astype(BF16)
    return high, (x - high.astype(F32)).astype(BF16)


def place(rel, order):
    pos = rel * 0
    for bit in order:
        pos = pos * 2 + ((rel >> bit) & 1)
    return pos


def bits_of(size):
    return list(range(size.bit_length() - 1))


def size_of(*shapes):
    total = 0
    for x in shapes:
        count = 1
        for d in x.shape:
            count *= d
        total += count * jnp.dtype(x.dtype).itemsize
    return total


def limit(*shapes):
    return min(size_of(*shapes) + (6 << 20), 60 << 20)


VMEM = pl.BlockSpec(memory_space=pltpu.VMEM)


def build_kernel(dims, x_hbm, ray_hbm, pix_hbm, slots_hbm, count_hbm, out_ref, *scratch):
    npix, nang, rays, own, pxd, blk, step = dims
    x_ref, ray_ref, pix_ref, slots_ref, count_ref, hot_ref, small_sem, x_sem = scratch
    slots = ray_ref.shape[1]
    pairs = nang * pxd // 2
    lanes = 2 * blk
    small = [
        pltpu.make_async_copy(source, target, small_sem.at[k])
        for k, (source, target) in enumerate(
            ((ray_hbm, ray_ref), (pix_hbm, pix_ref), (slots_hbm, slots_ref), (count_hbm, count_ref))
        )
    ]
    width = step * blk
    large = [
        pltpu.make_async_copy(x_hbm.at[:, pl.ds(k * width, width)], x_ref.at[:, pl.ds(k * width, width)], x_sem.at[k])
        for k in range(blk // step)
    ]
    for copy in small + large:
        copy.start()
    for copy in small:
        copy.wait()

    me, ang = lax.axis_index("pix"), lax.axis_index("ang")
    ray = ray_ref[...]
    slot = jnp.zeros_like(ray)
    for r in range(rays):
        slot = jnp.where(ray == r, slots_ref[0, r], slot)
    rel = (slot // own) ^ me
    pos = (rel % 8) * (npix // 8) + rel // 8
    row = pos * own + slot % own
    pix = pix_ref[...]
    column = place((pix // pxd) ^ ang, bits_of(nang)) * pxd + pix % pxd
    block = (column // 2) * (2 * rays) + (column % 2) * rays + row
    number = lax.broadcasted_iota(jnp.int32, (1, slots), 1)
    block = jnp.where(number < count_ref[0, 0], block, -1)
    rows = lax.broadcasted_iota(jnp.int32, (2 * pairs * rays, slots), 0)
    hot_ref[...] = (rows == block).astype(F32).astype(BF16)

    pack = rays // 8
    left = lax.broadcasted_iota(jnp.int32, (rays, lanes), 1) < blk
    above = lax.broadcasted_iota(jnp.int32, (pack, 8, lanes), 1) < 4

    def rows_of(sums, p, k):
        even = sums[2 * p * rays : (2 * p + 1) * rays, k * lanes : (k + 1) * lanes]
        odd = sums[(2 * p + 1) * rays : (2 * p + 2) * rays, k * lanes : (k + 1) * lanes]
        upper = jnp.where(left, even, pltpu.roll(odd, blk, 1)).reshape(pack, 8, lanes)
        lower = jnp.where(left, pltpu.roll(even, blk, 1), odd).reshape(pack, 8, lanes)
        return jnp.where(above, upper, pltpu.roll(lower, 4, 1)), jnp.where(above, pltpu.roll(upper, 4, 1), lower)

    for n in range(blk // step):
        large[n].wait()
        for g in range(step // 4):
            start = n * width + g * 2 * lanes
            high, low = split(x_ref[:, start : start + 2 * lanes])
            hot = hot_ref[...]
            sums = jnp.dot(hot, high, preferred_element_type=F32) + jnp.dot(hot, low, preferred_element_type=F32)
            at = 16 * (n * step // 4 + g)
            for p in range(pairs):
                for owner, value in enumerate(zip(rows_of(sums, p, 0), rows_of(sums, p, 1), strict=True)):
                    high, low = split(jnp.concatenate(value, axis=1))
                    out_ref[:, owner, at : at + 16, p * lanes : (p + 1) * lanes] = high
                    out_ref[:, owner, at : at + 16, (pairs + p) * lanes : (pairs + p + 1) * lanes] = low


def build(tiles, tile_ray, tile_pix, ray_slot, tile_count, dims):
    npix, nang, rays, own, pxd, blk, step = dims
    slots = tiles.shape[0]
    assert own == 4 and npix % 8 == 0 and pxd == 2
    columns = nang * pxd * blk
    shape = jax.ShapeDtypeStruct((npix // 2, 2, own * blk, 2 * columns), BF16)
    hot = jax.ShapeDtypeStruct((nang * pxd * rays, slots), BF16)
    hbm = pl.BlockSpec(memory_space=pltpu.HBM)
    small = size_of(shape) <= 6 << 20
    grant = 58 << 20 if small else limit(tiles, shape, hot)
    return pl.pallas_call(
        functools.partial(build_kernel, dims),
        in_specs=[hbm] * 5,
        out_specs=VMEM,
        out_shape=pltpu.VMEM(shape.shape, BF16) if small else shape,
        scratch_shapes=[
            pltpu.VMEM(tiles.shape, F32),
            pltpu.VMEM(tile_ray.shape, jnp.int32),
            pltpu.VMEM(tile_pix.shape, jnp.int32),
            pltpu.SMEM(ray_slot.shape, jnp.int32),
            pltpu.SMEM(tile_count.shape, jnp.int32),
            pltpu.VMEM(hot.shape, BF16),
            pltpu.SemaphoreType.DMA((4,)),
            pltpu.SemaphoreType.DMA((blk // step,)),
        ],
        compiler_params=pltpu.CompilerParams(vmem_limit_bytes=grant),
        cost_estimate=pl.CostEstimate(
            flops=4 * nang * pxd * rays * slots * blk * blk, bytes_accessed=tiles.size * 4 + 4 * rays * blk * columns, transcendentals=0
        ),
        name="build",
    )(tiles, tile_ray, tile_pix, ray_slot, tile_count).reshape(rays * blk, 2 * columns)


def loop(count, body):
    if count <= 16:
        for k in range(count):
            body(k)
    else:
        lax.fori_loop(0, count, lambda k, c: (body(k), c)[1], 0)


NT = (((1,), (1,)), ((), ()))


def project(lhs_ref, dense_ref, out_ref, start):
    pieces, tall, half = out_ref.shape
    s = (tall - EXTRA) // 2
    piece = 2 * half

    def body(k):
        rows = pl.ds(start + k * piece, piece)
        r = lax.dot_general(lhs_ref[...], dense_ref[rows, :], NT, preferred_element_type=F32)
        for h in range(2):
            part = r[:, h * half : (h + 1) * half]
            out_ref[k, h * s : (h + 1) * s, :] = part[:s] + part[s : 2 * s]
            out_ref[k, 2 * s + h : 2 * s + EXTRA, :] = part[2 * s : 2 * s + EXTRA - h]

    loop(pieces, body)


def forward_first_kernel(parts, groups, *refs):
    images, (dense_ref, *outs, lhs_ref) = refs[: len(parts)], refs[len(parts) :]
    columns = lhs_ref.shape[1] // 2
    for place_of, image_ref in zip(parts, images, strict=True):
        width, s = image_ref.shape
        high, low = split(image_ref[...].T)
        for at in (place_of * width, columns + place_of * width):
            lhs_ref[:s, at : at + width] = high
            lhs_ref[s : 2 * s, at : at + width] = low
    lhs_ref[2 * s :, :] = jnp.ones((2 * EXTRA, lhs_ref.shape[1]), BF16)
    for g, out_ref in zip(groups, outs, strict=True):
        project(lhs_ref, dense_ref, out_ref, g * (dense_ref.shape[0] // 8))


def forward_rest_kernel(groups, lhs_ref, dense_ref, *outs):
    for g, out_ref in zip(groups, outs, strict=True):
        project(lhs_ref, dense_ref, out_ref, g * (dense_ref.shape[0] // 8))


def forward(images, parts, dense, piece, first, rest):
    s = images[0].shape[1]
    rows, columns = dense.shape
    out = jax.ShapeDtypeStruct((rows // piece // 8, 2 * s + EXTRA, piece // 2), F32)
    lhs = jax.ShapeDtypeStruct((2 * s + 2 * EXTRA, columns), BF16)
    params = pltpu.CompilerParams(vmem_limit_bytes=limit(dense, lhs, *images, *[out] * len(rest)))

    def cost(groups):
        return pl.CostEstimate(
            flops=len(groups) * rows * columns * s // 2, bytes_accessed=len(groups) * rows * columns // 4, transcendentals=0
        )

    *early, lhs = pl.pallas_call(
        functools.partial(forward_first_kernel, parts, first),
        in_specs=[VMEM] * (1 + len(images)),
        out_specs=[VMEM] * (len(first) + 1),
        out_shape=[out] * len(first) + [lhs],
        cost_estimate=cost(first),
        compiler_params=params,
        name="forward_first",
    )(*images, dense)
    late = pl.pallas_call(
        functools.partial(forward_rest_kernel, rest),
        in_specs=[VMEM] * 2,
        out_specs=[VMEM] * len(rest),
        out_shape=[out] * len(rest),
        cost_estimate=cost(rest),
        compiler_params=params,
        name="forward_rest",
    )(lhs, dense)
    return dict(zip([*first, *rest], [*early, *late], strict=True))


def spread(resid_ref, dense_ref, start, total):
    pieces, piece, s = resid_ref.shape[0], 2 * resid_ref.shape[2], resid_ref.shape[1] // 2
    columns = total.shape[1]
    ones = jnp.ones((2 * EXTRA, piece), BF16)

    def body(k):
        resid = jnp.concatenate([resid_ref[k, :s], resid_ref[k, s:]], axis=1)
        lhs = jnp.concatenate([*split(resid), ones], axis=0)
        rows = pl.ds(start + k * piece, piece)
        both = jnp.concatenate([dense_ref[rows, :columns], dense_ref[rows, columns:]], axis=0)
        total[...] += jnp.dot(jnp.concatenate([lhs, lhs], axis=1), both, preferred_element_type=F32)

    loop(pieces, body)


def backward_kernel(groups, first, last, *refs):
    resids, (dense_ref, *rest) = refs[: len(groups)], refs[len(groups) :]
    total = rest[-1]
    total[...] = jnp.zeros_like(total) if first else rest[0][...]
    for g, resid_ref in zip(groups, resids, strict=True):
        spread(resid_ref, dense_ref, g * (dense_ref.shape[0] // 8), total)
    if last:
        kept_ref, sent_ref = rest[-3:-1]
        pieces, tall, width = kept_ref.shape
        s = tall - EXTRA
        for p in range(2 * pieces):
            out_ref, k = (kept_ref, p) if p < pieces else (sent_ref, p - pieces)
            part = total[:, p * width : (p + 1) * width]
            out_ref[k, :s, :] = part[:s] + part[s : 2 * s]
            out_ref[k, s:, :] = part[2 * s : 2 * s + EXTRA]


def backward(resids, dense, parts, before, last):
    s = next(iter(resids.values())).shape[1] // 2
    rows, columns = dense.shape[0], dense.shape[1] // 2
    total = jax.ShapeDtypeStruct((2 * s + 2 * EXTRA, columns), F32)
    out = jax.ShapeDtypeStruct((parts // 2, s + EXTRA, columns // parts), F32)
    operands = [*resids.values(), dense] + ([] if before is None else [before])
    return pl.pallas_call(
        functools.partial(backward_kernel, list(resids), before is None, last),
        in_specs=[VMEM] * len(operands),
        out_specs=[VMEM] * 2 if last else VMEM,
        out_shape=[out, out] if last else total,
        scratch_shapes=[pltpu.VMEM(total.shape, F32)] if last else [],
        cost_estimate=pl.CostEstimate(
            flops=len(resids) * rows * columns * s, bytes_accessed=len(resids) * rows * columns // 2, transcendentals=0
        ),
        compiler_params=pltpu.CompilerParams(vmem_limit_bytes=limit(total, total, *operands)),
        name="backward",
    )(*operands)


def prepare_kernel(own, measured_ref, out_ref, rows_ref):
    blk, half = measured_ref.shape[0] // own, out_ref.shape[1]
    s = out_ref.shape[0] // 2
    for r in range(own):
        rows_ref[pl.ds(r, blk, stride=own), :] = measured_ref[r * blk : (r + 1) * blk, :]
    for h in range(2):
        out_ref[h * s : (h + 1) * s, :] = rows_ref[h * half : (h + 1) * half, :].T


def restore_kernel(own, resid_ref, out_ref, rows_ref):
    blk, half = out_ref.shape[0] // own, resid_ref.shape[1]
    s = resid_ref.shape[0] // 2
    for h in range(2):
        rows_ref[h * half : (h + 1) * half, :] = resid_ref[h * s : (h + 1) * s, :].T
    for r in range(own):
        out_ref[r * blk : (r + 1) * blk, :] = rows_ref[pl.ds(r, blk, stride=own), :]


def turn(kernel, own, x, out, rows):
    return pl.pallas_call(
        functools.partial(kernel, own),
        in_specs=[VMEM],
        out_specs=VMEM,
        out_shape=jax.ShapeDtypeStruct(out, F32),
        scratch_shapes=[pltpu.VMEM(rows, F32)],
        compiler_params=pltpu.CompilerParams(vmem_limit_bytes=limit(x, x)),
        cost_estimate=pl.CostEstimate(flops=x.size, bytes_accessed=8 * x.size, transcendentals=0),
    )(x)


def swap(x, axis, mask):
    return lax.ppermute(x, axis, [(i, i ^ mask) for i in range(lax.axis_size(axis))])


def shards(tiles, tile_ray, tile_pix, tile_count, ray_slot, image, measured):
    npix, nang = lax.axis_size("pix"), lax.axis_size("ang")
    rays, slots = ray_slot.shape[1], tiles.shape[2]
    own = rays // npix
    blk = measured.shape[1] // own
    s = image.shape[1]
    pxd = image.shape[0] // blk
    dims = (npix, nang, rays, own, pxd, blk, 16)
    piece = own * blk
    more = bits_of(npix)[3:]

    images = [image] + [swap(image, "ang", r) for r in range(1, nang)]
    dense = build(tiles.reshape(slots, blk * blk), tile_ray[0], tile_pix[0], ray_slot, tile_count, dims)
    parts = [int(place(np.int32(r), bits_of(nang))) for r in range(nang)]

    proj = forward(images, parts, dense, piece, [7, 5, 6], [1, 2, 3, 4, 0])
    far = [swap(proj[4 + d], "pix", d) for d in (2, 1, 3)]
    crossing = swap(proj[4] + far[0] + far[1] + far[2], "pix", 4)
    near = [swap(proj[d], "pix", d) for d in (1, 2, 3)]
    total = proj[0] + near[0] + near[1] + near[2] + crossing
    for bit in reversed(more):
        m = total.shape[0] // 2
        total = total[:m] + swap(total[m:], "pix", 1 << bit)
    total = total[0]
    straight, turned = (piece, s), (2 * s, piece // 2)
    wanted = turn(prepare_kernel, own, measured[0], turned, straight)
    resid = jnp.concatenate(
        [(wanted[h * s : (h + 1) * s] - total[h * s : (h + 1) * s]) / total[2 * s + h][None] for h in range(2)]
    )
    resid_own = turn(restore_kernel, own, resid, straight, straight)[None]

    held = resid[None]
    for bit in more:
        held = jnp.concatenate([held, swap(held, "pix", 1 << bit)])
    got = {0: held, 4: swap(held, "pix", 4)}
    for d in (1, 2, 3):
        got[d] = swap(held, "pix", d)
    for d in (2, 1, 3):
        got[4 + d] = swap(got[4], "pix", d)
    turns = [(0, 1, 2, 3), (4, 7), (5,), (6,)]
    back = None
    for k, groups in enumerate(turns):
        back = backward({g: got[g] for g in groups}, dense, nang, back, k == len(turns) - 1)
    kept, sent = back
    for bit in bits_of(nang):
        arrived = swap(sent, "ang", 1 << bit)
        m = kept.shape[0] // 2
        kept, sent = (kept[:m] + arrived[:m], kept[m:] + arrived[m:]) if m else (kept + arrived, None)
    back = kept[0]
    new_image = image + RELAX * (back[:s] / back[s : s + 1]).T
    return new_image, resid_own


def solution(mesh):
    in_specs = (
        P("pix", "ang", None, None),
        P("pix", "ang", None),
        P("pix", "ang", None),
        P("pix", "ang"),
        P("ang", None),
        P(("pix", "ang"), None),
        P("ang", "pix", None),
    )
    out_specs = (P(("pix", "ang"), None), P("ang", "pix", None))
    return jax.shard_map(shards, mesh=mesh, in_specs=in_specs, out_specs=out_specs, check_vma=False)
```

profile of v0, /device:TPU:0, one launch (start us, length us, event | category | flops | bytes accessed | tf_op | source)
XLA Modules:
  0.0 53.7 jit_solution(983289651039787396)
XLA Ops:
  0.6 0.6 %collective-permute-start = (f32[128,128]{1,0:T(8,128)}, f32[128,128]{1,0:T(8,128)S(1)}, u32[]{:S(2)}, u32[]{:S(2)}) collective-permute-start(f32[128,128]{1,0:T(8,128)} %refs_0_.1), channel_id=1, source_target_pairs={{0,1},{1,0},{2,3},{3,2},{4,5},{5,4},{6,7},{7,6},{8,9},{9,8},{10,11... | collective-permute-start | bytes 196616 | tf_op jit(solution)/shard_map/ppermute | solution.py:310
  1.2 2.6 %collective-permute-start.1 = (f32[128,128]{1,0:T(8,128)}, f32[128,128]{1,0:T(8,128)S(1)}, u32[]{:S(2)}, u32[]{:S(2)}) collective-permute-start(f32[128,128]{1,0:T(8,128)} %refs_0_.1), channel_id=1, source_target_pairs={{0,2},{1,3},{2,0},{3,1},{4,6},{5,7},{6,4},{7,5},{8,10},{9,11},{10,... | collective-permute-start | bytes 196616 | tf_op jit(solution)/shard_map/ppermute | solution.py:310
  4.5 5.5 %build.1 = bf16[4,2,256,1024]{3,2,1,0:T(8,128)(2,1)S(1)} custom-call(f32[512,4096]{1,0:T(8,128)} %bitcast.47, s32[1,512]{1,0:T(1,128)} %bitcast.49, s32[1,512]{1,0:T(1,128)} %bitcast.50, s32[1,32]{1,0:T(1,128)} %slots_hbm.1, s32[1,1]{1,0:T(1,128)S(6)} %copy.11.count_hbm), custom_call_target="tpu_custom_call" | custom-call | flops 2147483648 | bytes 12582912 | tf_op jit(solution)/shard_map/build/pallas_call | solution.py:125
  10.0 0.7 %forward_first.1 = (f32[1,264,128]{2,1,0:T(8,128)S(1)}, f32[1,264,128]{2,1,0:T(8,128)S(1)}, f32[1,264,128]{2,1,0:T(8,128)S(1)}, bf16[272,1024]{1,0:T(8,128)(2,1)S(1)}) custom-call(f32[128,128]{1,0:T(8,128)S(1)} %copy-done, f32[128,128]{1,0:T(8,128)S(1)} %collective-permute-done.refs_1_, f32[128,128]{1,0:T(8,128)S(1)} %collective-permute-done.1.refs_2_, ...), custom_call_target="tpu_custom_call" | custom-call | flops 402653184 | bytes 1572864 | tf_op jit(solution)/shard_map/forward_first/pallas_call | solution.py:206
  10.7 1.9 %collective-permute-start.6 = (f32[1,264,128]{2,1,0:T(8,128)S(1)}, f32[1,264,128]{2,1,0:T(8,128)S(1)}, u32[]{:S(2)}, u32[]{:S(2)}) collective-permute-start(f32[1,264,128]{2,1,0:T(8,128)S(1)} %get-tuple-element.19), channel_id=1, source_target_pairs={{0,8},{4,12},{8,0},{12,4},{16,24},{20,28},{24,16},{28,20},{1,9},{5... | collective-permute-start | bytes 405512 | tf_op jit(solution)/shard_map/ppermute | solution.py:310
  12.6 1.5 %collective-permute-start.7 = (f32[1,264,128]{2,1,0:T(8,128)S(1)}, f32[1,264,128]{2,1,0:T(8,128)S(1)}, u32[]{:S(2)}, u32[]{:S(2)}) collective-permute-start(f32[1,264,128]{2,1,0:T(8,128)S(1)} %get-tuple-element.20), channel_id=1, source_target_pairs={{0,4},{4,0},{8,12},{12,8},{16,20},{20,16},{24,28},{28,24},{1,5},{5... | collective-permute-start | bytes 405512 | tf_op jit(solution)/shard_map/ppermute | solution.py:310
  14.2 0.9 %forward_rest.1 = (f32[1,264,128]{2,1,0:T(8,128)S(1)}, f32[1,264,128]{2,1,0:T(8,128)S(1)}, f32[1,264,128]{2,1,0:T(8,128)S(1)}, f32[1,264,128]{2,1,0:T(8,128)S(1)}, f32[1,264,128]{2,1,0:T(8,128)S(1)}) custom-call(bf16[272,1024]{1,0:T(8,128)(2,1)S(1)} %get-tuple-element.13.lhs_ref, bf16[2048,1024]{1,0:T(8,128)(2,1)S(1)} %bitcast.41), custom_call_target="tpu_custom_call" | custom-call | flops 671088640 | bytes 2621440 | tf_op jit(solution)/shard_map/forward_rest/pallas_call | solution.py:215
  15.2 1.8 %collective-permute-start.3 = (f32[1,264,128]{2,1,0:T(8,128)S(1)}, f32[1,264,128]{2,1,0:T(8,128)S(1)}, u32[]{:S(2)}, u32[]{:S(2)}) collective-permute-start(f32[1,264,128]{2,1,0:T(8,128)S(1)} %get-tuple-element.15), channel_id=1, source_target_pairs={{0,4},{4,0},{8,12},{12,8},{16,20},{20,16},{24,28},{28,24},{1,5},{5... | collective-permute-start | bytes 405512 | tf_op jit(solution)/shard_map/ppermute | solution.py:310
  17.0 1.6 %collective-permute-start.4 = (f32[1,264,128]{2,1,0:T(8,128)S(1)}, f32[1,264,128]{2,1,0:T(8,128)S(1)}, u32[]{:S(2)}, u32[]{:S(2)}) collective-permute-start(f32[1,264,128]{2,1,0:T(8,128)S(1)} %get-tuple-element.16), channel_id=1, source_target_pairs={{0,8},{4,12},{8,0},{12,4},{16,24},{20,28},{24,16},{28,20},{1,9},{5... | collective-permute-start | bytes 405512 | tf_op jit(solution)/shard_map/ppermute | solution.py:310
  18.6 1.4 %collective-permute-start.5 = (f32[1,264,128]{2,1,0:T(8,128)S(1)}, f32[1,264,128]{2,1,0:T(8,128)S(1)}, u32[]{:S(2)}, u32[]{:S(2)}) collective-permute-start(f32[1,264,128]{2,1,0:T(8,128)S(1)} %get-tuple-element.17), channel_id=1, source_target_pairs={{0,12},{4,8},{8,4},{12,0},{16,28},{20,24},{24,20},{28,16},{1,13},{... | collective-permute-start | bytes 405512 | tf_op jit(solution)/shard_map/ppermute | solution.py:310
  20.0 1.8 %collective-permute-done.7 = f32[1,264,128]{2,1,0:T(8,128)S(1)} collective-permute-done((f32[1,264,128]{2,1,0:T(8,128)S(1)}, f32[1,264,128]{2,1,0:T(8,128)S(1)}, u32[]{:S(2)}, u32[]{:S(2)}) %collective-permute-start.7) | collective-permute-done | bytes 135200 | tf_op jit(solution)/shard_map/ppermute | solution.py:310
  21.8 2.6 %collective-permute-start.9 = (f32[1,264,128]{2,1,0:T(8,128)S(1)}, f32[1,264,128]{2,1,0:T(8,128)S(1)}, u32[]{:S(2)}, u32[]{:S(2)}) collective-permute-start(f32[1,264,128]{2,1,0:T(8,128)S(1)} %add_add_fusion), channel_id=1, source_target_pairs={{0,16},{4,20},{8,24},{12,28},{16,0},{20,4},{24,8},{28,12},{1,17},{... | collective-permute-start | bytes 405512 | tf_op jit(solution)/shard_map/ppermute | solution.py:310
  24.5 0.5 collective-permute-done.3
  25.0 3.1 %collective-permute-done.5 = f32[1,264,128]{2,1,0:T(8,128)S(1)} collective-permute-done((f32[1,264,128]{2,1,0:T(8,128)S(1)}, f32[1,264,128]{2,1,0:T(8,128)S(1)}, u32[]{:S(2)}, u32[]{:S(2)}) %collective-permute-start.5) | collective-permute-done | bytes 135200 | tf_op jit(solution)/shard_map/ppermute | solution.py:310
  28.1 2.6 %collective-permute-done.9 = f32[1,264,128]{2,1,0:T(8,128)S(1)} collective-permute-done((f32[1,264,128]{2,1,0:T(8,128)S(1)}, f32[1,264,128]{2,1,0:T(8,128)S(1)}, u32[]{:S(2)}, u32[]{:S(2)}) %collective-permute-start.9) | collective-permute-done | bytes 135200 | tf_op jit(solution)/shard_map/ppermute | solution.py:310
  30.8 0.5 collective-permute-start.10
  31.3 2.0 %collective-permute-start.14 = (f32[1,256,128]{2,1,0:T(8,128)S(1)}, f32[1,256,128]{2,1,0:T(8,128)S(1)}, u32[]{:S(2)}, u32[]{:S(2)}) collective-permute-start(f32[1,256,128]{2,1,0:T(8,128)S(1)} %get-tuple-element.31.refs_0_), channel_id=1, source_target_pairs={{0,4},{4,0},{8,12},{12,8},{16,20},{20,16},{24,28},{28,24},{1,5},{5... | collective-permute-start | bytes 393224 | tf_op jit(solution)/shard_map/ppermute | solution.py:310
  33.3 1.8 %collective-permute-start.15 = (f32[1,256,128]{2,1,0:T(8,128)S(1)}, f32[1,256,128]{2,1,0:T(8,128)S(1)}, u32[]{:S(2)}, u32[]{:S(2)}) collective-permute-start(f32[1,256,128]{2,1,0:T(8,128)S(1)} %get-tuple-element.31.refs_0_), channel_id=1, source_target_pairs={{0,8},{4,12},{8,0},{12,4},{16,24},{20,28},{24,16},{28,20},{1,9},{5... | collective-permute-start | bytes 393224 | tf_op jit(solution)/shard_map/ppermute | solution.py:310
  35.5 2.6 %collective-permute-done.10.refs_0_ = f32[1,256,128]{2,1,0:T(8,128)S(1)} collective-permute-done((f32[1,256,128]{2,1,0:T(8,128)S(1)}, f32[1,256,128]{2,1,0:T(8,128)S(1)}, u32[]{:S(2)}, u32[]{:S(2)}) %collective-permute-start.10) | collective-permute-done | bytes 131104 | tf_op jit(solution)/shard_map/ppermute | solution.py:310
  38.1 1.5 %collective-permute-start.13 = (f32[1,256,128]{2,1,0:T(8,128)S(1)}, f32[1,256,128]{2,1,0:T(8,128)S(1)}, u32[]{:S(2)}, u32[]{:S(2)}) collective-permute-start(f32[1,256,128]{2,1,0:T(8,128)S(1)} %collective-permute-done.10.refs_0_), channel_id=1, source_target_pairs={{0,12},{4,8},{8,4},{12,0},{16,28},{20,24},{24,20},{28,16},{1,13},{... | collective-permute-start | bytes 393224 | tf_op jit(solution)/shard_map/ppermute | solution.py:310
  39.6 0.5 collective-permute-start.12
  40.1 1.5 %collective-permute-start.11 = (f32[1,256,128]{2,1,0:T(8,128)S(1)}, f32[1,256,128]{2,1,0:T(8,128)S(1)}, u32[]{:S(2)}, u32[]{:S(2)}) collective-permute-start(f32[1,256,128]{2,1,0:T(8,128)S(1)} %collective-permute-done.10.refs_0_), channel_id=1, source_target_pairs={{0,8},{4,12},{8,0},{12,4},{16,24},{20,28},{24,16},{28,20},{1,9},{5... | collective-permute-start | bytes 393224 | tf_op jit(solution)/shard_map/ppermute | solution.py:310
  41.6 2.4 %collective-permute-done.16.refs_3_ = f32[1,256,128]{2,1,0:T(8,128)S(1)} collective-permute-done((f32[1,256,128]{2,1,0:T(8,128)S(1)}, f32[1,256,128]{2,1,0:T(8,128)S(1)}, u32[]{:S(2)}, u32[]{:S(2)}) %collective-permute-start.16) | collective-permute-done | bytes 131104 | tf_op jit(solution)/shard_map/ppermute | solution.py:310
  44.0 0.7 %backward.4.refs_3_ = f32[272,512]{1,0:T(8,128)S(1)} custom-call(f32[1,256,128]{2,1,0:T(8,128)S(1)} %get-tuple-element.31.refs_0_, f32[1,256,128]{2,1,0:T(8,128)S(1)} %collective-permute-done.14.refs_1_, f32[1,256,128]{2,1,0:T(8,128)S(1)} %collective-permute-done.15.refs_2_, f32[1,256,128]{2,1,0:T(8,128)S(1)} %collective-permute-done.16.refs_3_, ...), custom_call_target="tpu_custom_call" | custom-call | flops 536870912 | bytes 2097152 | tf_op jit(solution)/shard_map/backward/pallas_call | solution.py:265
  44.7 0.8 %collective-permute-done.13.refs_1_ = f32[1,256,128]{2,1,0:T(8,128)S(1)} collective-permute-done((f32[1,256,128]{2,1,0:T(8,128)S(1)}, f32[1,256,128]{2,1,0:T(8,128)S(1)}, u32[]{:S(2)}, u32[]{:S(2)}) %collective-permute-start.13) | collective-permute-done | bytes 131104 | tf_op jit(solution)/shard_map/ppermute | solution.py:310
  45.5 0.5 backward.5.refs_2_
  46.0 0.4 collective-permute-done.12.refs_0_
  47.2 1.3 %collective-permute-done.17 = f32[2,136,128]{2,1,0:T(8,128)S(1)} collective-permute-done((f32[2,136,128]{2,1,0:T(8,128)S(1)}, f32[2,136,128]{2,1,0:T(8,128)S(1)}, u32[]{:S(2)}, u32[]{:S(2)}) %collective-permute-start.17) | collective-permute-done | bytes 139296 | tf_op jit(solution)/shard_map/ppermute | solution.py:310
  48.5 1.4 %collective-permute-start.18 = (f32[1,136,128]{2,1,0:T(8,128)S(1)}, f32[1,136,128]{2,1,0:T(8,128)S(1)}, u32[]{:S(2)}, u32[]{:S(2)}) collective-permute-start(f32[1,136,128]{2,1,0:T(8,128)S(1)} %slice_add_fusion), channel_id=1, source_target_pairs={{0,2},{1,3},{2,0},{3,1},{4,6},{5,7},{6,4},{7,5},{8,10},{9,11},{10,... | collective-permute-start | bytes 208904 | tf_op jit(solution)/shard_map/ppermute | solution.py:310
  50.0 0.8 %shard_map.87 = f32[256,128]{1,0:T(8,128)} custom-call(f32[256,128]{1,0:T(8,128)S(1)} %get-tuple-element.30.resid_ref), custom_call_target="tpu_custom_call" | custom-call | flops 32768 | bytes 262144 | tf_op jit(solution)/shard_map/pallas_call | solution.py:298
  50.8 2.1 %collective-permute-done.18 = f32[1,136,128]{2,1,0:T(8,128)S(1)} collective-permute-done((f32[1,136,128]{2,1,0:T(8,128)S(1)}, f32[1,136,128]{2,1,0:T(8,128)S(1)}, u32[]{:S(2)}, u32[]{:S(2)}) %collective-permute-start.18) | collective-permute-done | bytes 69664 | tf_op jit(solution)/shard_map/ppermute | solution.py:310
  53.0 0.7 %copy.10 = f32[128,128]{1,0:T(8,128)} copy(f32[128,128]{0,1:T(8,128)S(1)} %fusion.4) | data formatting | bytes 131072
  (30 shorter events, 1.7 us)
Async XLA Ops:
  0.6 9.4 %copy-start = (f32[128,128]{1,0:T(8,128)S(1)}, f32[128,128]{1,0:T(8,128)}, u32[]{:S(2)}) copy-start(f32[128,128]{1,0:T(8,128)} %refs_0_.1) | copy-start | bytes 196612
  0.6 9.3 %collective-permute-start = (f32[128,128]{1,0:T(8,128)}, f32[128,128]{1,0:T(8,128)S(1)}, u32[]{:S(2)}, u32[]{:S(2)}) collective-permute-start(f32[128,128]{1,0:T(8,128)} %refs_0_.1), channel_id=1, source_target_pairs={{0,1},{1,0},{2,3},{3,2},{4,5},{5,4},{6,7},{7,6},{8,9},{9,8},{10,11... | collective-permute-start | bytes 196616 | tf_op jit(solution)/shard_map/ppermute | solution.py:310
  1.2 8.8 %collective-permute-start.1 = (f32[128,128]{1,0:T(8,128)}, f32[128,128]{1,0:T(8,128)S(1)}, u32[]{:S(2)}, u32[]{:S(2)}) collective-permute-start(f32[128,128]{1,0:T(8,128)} %refs_0_.1), channel_id=1, source_target_pairs={{0,2},{1,3},{2,0},{3,1},{4,6},{5,7},{6,4},{7,5},{8,10},{9,11},{10,... | collective-permute-start | bytes 196616 | tf_op jit(solution)/shard_map/ppermute | solution.py:310
  3.8 6.2 %collective-permute-start.2 = (f32[128,128]{1,0:T(8,128)}, f32[128,128]{1,0:T(8,128)S(1)}, u32[]{:S(2)}, u32[]{:S(2)}) collective-permute-start(f32[128,128]{1,0:T(8,128)} %refs_0_.1), channel_id=1, source_target_pairs={{0,3},{1,2},{2,1},{3,0},{4,7},{5,6},{6,5},{7,4},{8,11},{9,10},{10,... | collective-permute-start | bytes 196616 | tf_op jit(solution)/shard_map/ppermute | solution.py:310
  4.4 20.0 %copy-start.1 = (f32[1,256,128]{2,1,0:T(8,128)S(1)}, f32[1,256,128]{2,1,0:T(8,128)}, u32[]{:S(2)}) copy-start(f32[1,256,128]{2,1,0:T(8,128)} %param.13) | copy-start | bytes 393220
  10.7 7.9 %collective-permute-start.6 = (f32[1,264,128]{2,1,0:T(8,128)S(1)}, f32[1,264,128]{2,1,0:T(8,128)S(1)}, u32[]{:S(2)}, u32[]{:S(2)}) collective-permute-start(f32[1,264,128]{2,1,0:T(8,128)S(1)} %get-tuple-element.19), channel_id=1, source_target_pairs={{0,8},{4,12},{8,0},{12,4},{16,24},{20,28},{24,16},{28,20},{1,9},{5... | collective-permute-start | bytes 405512 | tf_op jit(solution)/shard_map/ppermute | solution.py:310
  12.6 9.2 %collective-permute-start.7 = (f32[1,264,128]{2,1,0:T(8,128)S(1)}, f32[1,264,128]{2,1,0:T(8,128)S(1)}, u32[]{:S(2)}, u32[]{:S(2)}) collective-permute-start(f32[1,264,128]{2,1,0:T(8,128)S(1)} %get-tuple-element.20), channel_id=1, source_target_pairs={{0,4},{4,0},{8,12},{12,8},{16,20},{20,16},{24,28},{28,24},{1,5},{5... | collective-permute-start | bytes 405512 | tf_op jit(solution)/shard_map/ppermute | solution.py:310
  14.1 7.6 %collective-permute-start.8 = (f32[1,264,128]{2,1,0:T(8,128)S(1)}, f32[1,264,128]{2,1,0:T(8,128)S(1)}, u32[]{:S(2)}, u32[]{:S(2)}) collective-permute-start(f32[1,264,128]{2,1,0:T(8,128)S(1)} %get-tuple-element.21), channel_id=1, source_target_pairs={{0,12},{4,8},{8,4},{12,0},{16,28},{20,24},{24,20},{28,16},{1,13},{... | collective-permute-start | bytes 405512 | tf_op jit(solution)/shard_map/ppermute | solution.py:310
  15.2 9.8 %collective-permute-start.3 = (f32[1,264,128]{2,1,0:T(8,128)S(1)}, f32[1,264,128]{2,1,0:T(8,128)S(1)}, u32[]{:S(2)}, u32[]{:S(2)}) collective-permute-start(f32[1,264,128]{2,1,0:T(8,128)S(1)} %get-tuple-element.15), channel_id=1, source_target_pairs={{0,4},{4,0},{8,12},{12,8},{16,20},{20,16},{24,28},{28,24},{1,5},{5... | collective-permute-start | bytes 405512 | tf_op jit(solution)/shard_map/ppermute | solution.py:310
  17.0 8.0 %collective-permute-start.4 = (f32[1,264,128]{2,1,0:T(8,128)S(1)}, f32[1,264,128]{2,1,0:T(8,128)S(1)}, u32[]{:S(2)}, u32[]{:S(2)}) collective-permute-start(f32[1,264,128]{2,1,0:T(8,128)S(1)} %get-tuple-element.16), channel_id=1, source_target_pairs={{0,8},{4,12},{8,0},{12,4},{16,24},{20,28},{24,16},{28,20},{1,9},{5... | collective-permute-start | bytes 405512 | tf_op jit(solution)/shard_map/ppermute | solution.py:310
  18.6 9.5 %collective-permute-start.5 = (f32[1,264,128]{2,1,0:T(8,128)S(1)}, f32[1,264,128]{2,1,0:T(8,128)S(1)}, u32[]{:S(2)}, u32[]{:S(2)}) collective-permute-start(f32[1,264,128]{2,1,0:T(8,128)S(1)} %get-tuple-element.17), channel_id=1, source_target_pairs={{0,12},{4,8},{8,4},{12,0},{16,28},{20,24},{24,20},{28,16},{1,13},{... | collective-permute-start | bytes 405512 | tf_op jit(solution)/shard_map/ppermute | solution.py:310
  21.8 8.9 %collective-permute-start.9 = (f32[1,264,128]{2,1,0:T(8,128)S(1)}, f32[1,264,128]{2,1,0:T(8,128)S(1)}, u32[]{:S(2)}, u32[]{:S(2)}) collective-permute-start(f32[1,264,128]{2,1,0:T(8,128)S(1)} %add_add_fusion), channel_id=1, source_target_pairs={{0,16},{4,20},{8,24},{12,28},{16,0},{20,4},{24,8},{28,12},{1,17},{... | collective-permute-start | bytes 405512 | tf_op jit(solution)/shard_map/ppermute | solution.py:310
  30.8 7.3 %collective-permute-start.10 = (f32[1,256,128]{2,1,0:T(8,128)S(1)}, f32[1,256,128]{2,1,0:T(8,128)S(1)}, u32[]{:S(2)}, u32[]{:S(2)}) collective-permute-start(f32[1,256,128]{2,1,0:T(8,128)S(1)} %get-tuple-element.31.refs_0_), channel_id=1, source_target_pairs={{0,16},{4,20},{8,24},{12,28},{16,0},{20,4},{24,8},{28,12},{1,17},{... | collective-permute-start | bytes 393224 | tf_op jit(solution)/shard_map/ppermute | solution.py:310
  31.3 8.9 %collective-permute-start.14 = (f32[1,256,128]{2,1,0:T(8,128)S(1)}, f32[1,256,128]{2,1,0:T(8,128)S(1)}, u32[]{:S(2)}, u32[]{:S(2)}) collective-permute-start(f32[1,256,128]{2,1,0:T(8,128)S(1)} %get-tuple-element.31.refs_0_), channel_id=1, source_target_pairs={{0,4},{4,0},{8,12},{12,8},{16,20},{20,16},{24,28},{28,24},{1,5},{5... | collective-permute-start | bytes 393224 | tf_op jit(solution)/shard_map/ppermute | solution.py:310
  33.3 8.3 %collective-permute-start.15 = (f32[1,256,128]{2,1,0:T(8,128)S(1)}, f32[1,256,128]{2,1,0:T(8,128)S(1)}, u32[]{:S(2)}, u32[]{:S(2)}) collective-permute-start(f32[1,256,128]{2,1,0:T(8,128)S(1)} %get-tuple-element.31.refs_0_), channel_id=1, source_target_pairs={{0,8},{4,12},{8,0},{12,4},{16,24},{20,28},{24,16},{28,20},{1,9},{5... | collective-permute-start | bytes 393224 | tf_op jit(solution)/shard_map/ppermute | solution.py:310
  35.0 8.9 %collective-permute-start.16 = (f32[1,256,128]{2,1,0:T(8,128)S(1)}, f32[1,256,128]{2,1,0:T(8,128)S(1)}, u32[]{:S(2)}, u32[]{:S(2)}) collective-permute-start(f32[1,256,128]{2,1,0:T(8,128)S(1)} %get-tuple-element.31.refs_0_), channel_id=1, source_target_pairs={{0,12},{4,8},{8,4},{12,0},{16,28},{20,24},{24,20},{28,16},{1,13},{... | collective-permute-start | bytes 393224 | tf_op jit(solution)/shard_map/ppermute | solution.py:310
  38.1 7.4 %collective-permute-start.13 = (f32[1,256,128]{2,1,0:T(8,128)S(1)}, f32[1,256,128]{2,1,0:T(8,128)S(1)}, u32[]{:S(2)}, u32[]{:S(2)}) collective-permute-start(f32[1,256,128]{2,1,0:T(8,128)S(1)} %collective-permute-done.10.refs_0_), channel_id=1, source_target_pairs={{0,12},{4,8},{8,4},{12,0},{16,28},{20,24},{24,20},{28,16},{1,13},{... | collective-permute-start | bytes 393224 | tf_op jit(solution)/shard_map/ppermute | solution.py:310
  39.6 6.8 %collective-permute-start.12 = (f32[1,256,128]{2,1,0:T(8,128)S(1)}, f32[1,256,128]{2,1,0:T(8,128)S(1)}, u32[]{:S(2)}, u32[]{:S(2)}) collective-permute-start(f32[1,256,128]{2,1,0:T(8,128)S(1)} %collective-permute-done.10.refs_0_), channel_id=1, source_target_pairs={{0,4},{4,0},{8,12},{12,8},{16,20},{20,16},{24,28},{28,24},{1,5},{5... | collective-permute-start | bytes 393224 | tf_op jit(solution)/shard_map/ppermute | solution.py:310
  40.1 6.6 %collective-permute-start.11 = (f32[1,256,128]{2,1,0:T(8,128)S(1)}, f32[1,256,128]{2,1,0:T(8,128)S(1)}, u32[]{:S(2)}, u32[]{:S(2)}) collective-permute-start(f32[1,256,128]{2,1,0:T(8,128)S(1)} %collective-permute-done.10.refs_0_), channel_id=1, source_target_pairs={{0,8},{4,12},{8,0},{12,4},{16,24},{20,28},{24,16},{28,20},{1,9},{5... | collective-permute-start | bytes 393224 | tf_op jit(solution)/shard_map/ppermute | solution.py:310
  47.1 1.4 %collective-permute-start.17 = (f32[2,136,128]{2,1,0:T(8,128)S(1)}, f32[2,136,128]{2,1,0:T(8,128)S(1)}, u32[]{:S(2)}, u32[]{:S(2)}) collective-permute-start(f32[2,136,128]{2,1,0:T(8,128)S(1)} %get-tuple-element.23), channel_id=1, source_target_pairs={{0,1},{1,0},{2,3},{3,2},{4,5},{5,4},{6,7},{7,6},{8,9},{9,8},{10,11... | collective-permute-start | bytes 417800 | tf_op jit(solution)/shard_map/ppermute | solution.py:310
  48.5 4.4 %collective-permute-start.18 = (f32[1,136,128]{2,1,0:T(8,128)S(1)}, f32[1,136,128]{2,1,0:T(8,128)S(1)}, u32[]{:S(2)}, u32[]{:S(2)}) collective-permute-start(f32[1,136,128]{2,1,0:T(8,128)S(1)} %slice_add_fusion), channel_id=1, source_target_pairs={{0,2},{1,3},{2,0},{3,1},{4,6},{5,7},{6,4},{7,5},{8,10},{9,11},{10,... | collective-permute-start | bytes 208904 | tf_op jit(solution)/shard_map/ppermute | solution.py:310
where the time goes:
time: 53.8 us; the launch traced here: 53.7 us
  starting transfers between devices  23.8 us (44%)
  waiting for transfers between devices  17.7 us (33%)
  Pallas kernels  9.77 us (18%)
  between operations  1.47 us (3%)
  local copies, waits for them, and re-layouts  0.83 us (2%)
    ppermute x19, starting transfers between devices, swap(): lax.ppermute(x, axis, [(i, i ^ mask) for i in range(lax.axis_size(axis))])  23.8 us
    ppermute x19, waiting for transfers between devices, swap(): lax.ppermute(x, axis, [(i, i ^ mask) for i in range(lax.axis_size(axis))])  17.7 us
    pallas_call x1, Pallas kernels, build(): pl.pallas_call(functools.partial(build_kernel, dims), in_specs=[hbm] * 5,...  5.49 us
    pallas_call x4, Pallas kernels, backward(): pl.pallas_call(functools.partial(backward_kernel, list(resids), before is...  1.8 us
  transfers between devices with their start and end apart: 19, of which 11 were waited for; matrix products, arithmetic and copies ran while one was open for 0% of the time, Pallas kernels for 16%

commit v1 on v0

--- a/solution.py
+++ b/solution.py
@@ -276,6 +276,44 @@
     )(*operands)
 
 
+def finish_kernel(group, side, resid_ref, dense_ref, before_ref, out_ref, total_ref):
+    parts, tall, width = out_ref.shape
+    s, piece, columns = tall - EXTRA, 2 * resid_ref.shape[2], before_ref.shape[1]
+    ones = jnp.ones((2 * EXTRA, piece), BF16)
+    span = parts * width
+    total_ref[...] = before_ref[:, side * span : (side + 1) * span]
+
+    def body(k):
+        resid = jnp.concatenate([resid_ref[k, :s], resid_ref[k, s:]], axis=1)
+        lhs = jnp.concatenate([*split(resid), ones], axis=0)
+        rows = pl.ds(group * (dense_ref.shape[0] // 8) + k * piece, piece)
+        both = [dense_ref[rows, at + side * span : at + (side + 1) * span] for at in (0, columns)]
+        total_ref[...] += jnp.dot(
+            jnp.concatenate([lhs, lhs], axis=1), jnp.concatenate(both, axis=0), preferred_element_type=F32
+        )
+
+    loop(resid_ref.shape[0], body)
+    for p in range(parts):
+        part = total_ref[:, p * width : (p + 1) * width]
+        out_ref[p, :s, :] = part[:s] + part[s : 2 * s]
+        out_ref[p, s:, :] = part[2 * s : 2 * s + EXTRA]
+
+
+def finish(resid, group, dense, parts, before, side):
+    tall, columns = before.shape
+    s = resid.shape[1] // 2
+    return pl.pallas_call(
+        functools.partial(finish_kernel, group, side),
+        in_specs=[VMEM] * 3,
+        out_specs=VMEM,
+        out_shape=jax.ShapeDtypeStruct((parts // 2, s + EXTRA, columns // parts), F32),
+        scratch_shapes=[pltpu.VMEM((tall, columns // 2), F32)],
+        cost_estimate=pl.CostEstimate(flops=dense.size * s // 4, bytes_accessed=dense.size // 4, transcendentals=0),
+        compiler_params=pltpu.CompilerParams(vmem_limit_bytes=limit(before, before, resid, dense)),
+        name="finish",
+    )(resid, dense, before)
+
+
 def prepare_kernel(own, measured_ref, out_ref, rows_ref):
     blk, half = measured_ref.shape[0] // own, out_ref.shape[1]
     s = out_ref.shape[0] // 2
@@ -349,11 +387,11 @@
         got[d] = swap(held, "pix", d)
     for d in (2, 1, 3):
         got[4 + d] = swap(got[4], "pix", d)
-    turns = [(0, 1, 2, 3), (4, 7), (5,), (6,)]
     back = None
-    for k, groups in enumerate(turns):
-        back = backward({g: got[g] for g in groups}, dense, nang, back, k == len(turns) - 1)
-    kept, sent = back
+    for groups in ((0, 1, 2, 3), (4, 7), (5,)):
+        back = backward({g: got[g] for g in groups}, dense, nang, back, False)
+    sent = finish(got[6], 6, dense, nang, back, 1)
+    kept = finish(got[6], 6, dense, nang, back, 0)
     for bit in bits_of(nang):
         arrived = swap(sent, "ang", 1 << bit)
         m = kept.shape[0] // 2

time: 53.8 us -> 53.8 us (level)
    pallas_call x4 -> x3, Pallas kernels: 1.8 us -> 1.49 us  [backward(): pl.pallas_call(functools.partial(backward_kernel, list(resids), before is...]
  transfers between devices with their start and end apart: 19 -> 19, of which waited for: 11 -> 11; matrix products, arithmetic and copies ran while one was open for 0% -> 0% of each run, Pallas kernels for 16% -> 17%
where the time goes in v1:
time: 53.8 us; the launch traced here: 53.6 us
  starting transfers between devices  23.8 us (44%)
  waiting for transfers between devices  17.4 us (32%)
  Pallas kernels  9.95 us (18%)
  between operations  1.47 us (3%)
  local copies, waits for them, and re-layouts  0.84 us (2%)
    ppermute x19, starting transfers between devices, swap(): lax.ppermute(x, axis, [(i, i ^ mask) for i in range(lax.axis_size(axis))])  23.8 us
    ppermute x19, waiting for transfers between devices, swap(): lax.ppermute(x, axis, [(i, i ^ mask) for i in range(lax.axis_size(axis))])  17.4 us
    pallas_call x1, Pallas kernels, build(): pl.pallas_call(functools.partial(build_kernel, dims), in_specs=[hbm] * 5,...  5.49 us
    pallas_call x3, Pallas kernels, backward(): pl.pallas_call(functools.partial(backward_kernel, list(resids), before is...  1.49 us
  transfers between devices with their start and end apart: 19, of which 11 were waited for; matrix products, arithmetic and copies ran while one was open for 0% of the time, Pallas kernels for 17%

profile of v1, /device:TPU:0, one launch (start us, length us, event | category | flops | bytes accessed | tf_op | source)
XLA Modules:
  0.0 53.6 jit_solution(5650930417717801930)
XLA Ops:
  0.6 0.6 %collective-permute-start = (f32[128,128]{1,0:T(8,128)}, f32[128,128]{1,0:T(8,128)S(1)}, u32[]{:S(2)}, u32[]{:S(2)}) collective-permute-start(f32[128,128]{1,0:T(8,128)} %refs_0_.1), channel_id=1, source_target_pairs={{0,1},{1,0},{2,3},{3,2},{4,5},{5,4},{6,7},{7,6},{8,9},{9,8},{10,11... | collective-permute-start | bytes 196616 | tf_op jit(solution)/shard_map/ppermute | solution.py:348
  1.2 2.6 %collective-permute-start.1 = (f32[128,128]{1,0:T(8,128)}, f32[128,128]{1,0:T(8,128)S(1)}, u32[]{:S(2)}, u32[]{:S(2)}) collective-permute-start(f32[128,128]{1,0:T(8,128)} %refs_0_.1), channel_id=1, source_target_pairs={{0,2},{1,3},{2,0},{3,1},{4,6},{5,7},{6,4},{7,5},{8,10},{9,11},{10,... | collective-permute-start | bytes 196616 | tf_op jit(solution)/shard_map/ppermute | solution.py:348
  4.5 5.5 %build.1 = bf16[4,2,256,1024]{3,2,1,0:T(8,128)(2,1)S(1)} custom-call(f32[512,4096]{1,0:T(8,128)} %bitcast.48, s32[1,512]{1,0:T(1,128)} %bitcast.50, s32[1,512]{1,0:T(1,128)} %bitcast.51, s32[1,32]{1,0:T(1,128)} %slots_hbm.1, s32[1,1]{1,0:T(1,128)S(6)} %copy.11.count_hbm), custom_call_target="tpu_custom_call" | custom-call | flops 2147483648 | bytes 12582912 | tf_op jit(solution)/shard_map/build/pallas_call | solution.py:125
  10.0 0.7 %forward_first.1 = (f32[1,264,128]{2,1,0:T(8,128)S(1)}, f32[1,264,128]{2,1,0:T(8,128)S(1)}, f32[1,264,128]{2,1,0:T(8,128)S(1)}, bf16[272,1024]{1,0:T(8,128)(2,1)S(1)}) custom-call(f32[128,128]{1,0:T(8,128)S(1)} %copy-done, f32[128,128]{1,0:T(8,128)S(1)} %collective-permute-done.refs_1_, f32[128,128]{1,0:T(8,128)S(1)} %collective-permute-done.1.refs_2_, ...), custom_call_target="tpu_custom_call" | custom-call | flops 402653184 | bytes 1572864 | tf_op jit(solution)/shard_map/forward_first/pallas_call | solution.py:206
  10.7 1.9 %collective-permute-start.6 = (f32[1,264,128]{2,1,0:T(8,128)S(1)}, f32[1,264,128]{2,1,0:T(8,128)S(1)}, u32[]{:S(2)}, u32[]{:S(2)}) collective-permute-start(f32[1,264,128]{2,1,0:T(8,128)S(1)} %get-tuple-element.17), channel_id=1, source_target_pairs={{0,8},{4,12},{8,0},{12,4},{16,24},{20,28},{24,16},{28,20},{1,9},{5... | collective-permute-start | bytes 405512 | tf_op jit(solution)/shard_map/ppermute | solution.py:348
  12.6 1.5 %collective-permute-start.7 = (f32[1,264,128]{2,1,0:T(8,128)S(1)}, f32[1,264,128]{2,1,0:T(8,128)S(1)}, u32[]{:S(2)}, u32[]{:S(2)}) collective-permute-start(f32[1,264,128]{2,1,0:T(8,128)S(1)} %get-tuple-element.18), channel_id=1, source_target_pairs={{0,4},{4,0},{8,12},{12,8},{16,20},{20,16},{24,28},{28,24},{1,5},{5... | collective-permute-start | bytes 405512 | tf_op jit(solution)/shard_map/ppermute | solution.py:348
  14.2 0.9 %forward_rest.1 = (f32[1,264,128]{2,1,0:T(8,128)S(1)}, f32[1,264,128]{2,1,0:T(8,128)S(1)}, f32[1,264,128]{2,1,0:T(8,128)S(1)}, f32[1,264,128]{2,1,0:T(8,128)S(1)}, f32[1,264,128]{2,1,0:T(8,128)S(1)}) custom-call(bf16[272,1024]{1,0:T(8,128)(2,1)S(1)} %get-tuple-element.11.lhs_ref, bf16[2048,1024]{1,0:T(8,128)(2,1)S(1)} %bitcast.41), custom_call_target="tpu_custom_call" | custom-call | flops 671088640 | bytes 2621440 | tf_op jit(solution)/shard_map/forward_rest/pallas_call | solution.py:215
  15.2 1.8 %collective-permute-start.3 = (f32[1,264,128]{2,1,0:T(8,128)S(1)}, f32[1,264,128]{2,1,0:T(8,128)S(1)}, u32[]{:S(2)}, u32[]{:S(2)}) collective-permute-start(f32[1,264,128]{2,1,0:T(8,128)S(1)} %get-tuple-element.13), channel_id=1, source_target_pairs={{0,4},{4,0},{8,12},{12,8},{16,20},{20,16},{24,28},{28,24},{1,5},{5... | collective-permute-start | bytes 405512 | tf_op jit(solution)/shard_map/ppermute | solution.py:348
  17.0 1.6 %collective-permute-start.4 = (f32[1,264,128]{2,1,0:T(8,128)S(1)}, f32[1,264,128]{2,1,0:T(8,128)S(1)}, u32[]{:S(2)}, u32[]{:S(2)}) collective-permute-start(f32[1,264,128]{2,1,0:T(8,128)S(1)} %get-tuple-element.14), channel_id=1, source_target_pairs={{0,8},{4,12},{8,0},{12,4},{16,24},{20,28},{24,16},{28,20},{1,9},{5... | collective-permute-start | bytes 405512 | tf_op jit(solution)/shard_map/ppermute | solution.py:348
  18.6 1.4 %collective-permute-start.5 = (f32[1,264,128]{2,1,0:T(8,128)S(1)}, f32[1,264,128]{2,1,0:T(8,128)S(1)}, u32[]{:S(2)}, u32[]{:S(2)}) collective-permute-start(f32[1,264,128]{2,1,0:T(8,128)S(1)} %get-tuple-element.15), channel_id=1, source_target_pairs={{0,12},{4,8},{8,4},{12,0},{16,28},{20,24},{24,20},{28,16},{1,13},{... | collective-permute-start | bytes 405512 | tf_op jit(solution)/shard_map/ppermute | solution.py:348
  20.0 1.8 %collective-permute-done.7 = f32[1,264,128]{2,1,0:T(8,128)S(1)} collective-permute-done((f32[1,264,128]{2,1,0:T(8,128)S(1)}, f32[1,264,128]{2,1,0:T(8,128)S(1)}, u32[]{:S(2)}, u32[]{:S(2)}) %collective-permute-start.7) | collective-permute-done | bytes 135200 | tf_op jit(solution)/shard_map/ppermute | solution.py:348
  21.8 2.6 %collective-permute-start.9 = (f32[1,264,128]{2,1,0:T(8,128)S(1)}, f32[1,264,128]{2,1,0:T(8,128)S(1)}, u32[]{:S(2)}, u32[]{:S(2)}) collective-permute-start(f32[1,264,128]{2,1,0:T(8,128)S(1)} %add_add_fusion), channel_id=1, source_target_pairs={{0,16},{4,20},{8,24},{12,28},{16,0},{20,4},{24,8},{28,12},{1,17},{... | collective-permute-start | bytes 405512 | tf_op jit(solution)/shard_map/ppermute | solution.py:348
  24.5 0.5 collective-permute-done.3
  25.0 3.1 %collective-permute-done.5 = f32[1,264,128]{2,1,0:T(8,128)S(1)} collective-permute-done((f32[1,264,128]{2,1,0:T(8,128)S(1)}, f32[1,264,128]{2,1,0:T(8,128)S(1)}, u32[]{:S(2)}, u32[]{:S(2)}) %collective-permute-start.5) | collective-permute-done | bytes 135200 | tf_op jit(solution)/shard_map/ppermute | solution.py:348
  28.1 2.6 %collective-permute-done.9 = f32[1,264,128]{2,1,0:T(8,128)S(1)} collective-permute-done((f32[1,264,128]{2,1,0:T(8,128)S(1)}, f32[1,264,128]{2,1,0:T(8,128)S(1)}, u32[]{:S(2)}, u32[]{:S(2)}) %collective-permute-start.9) | collective-permute-done | bytes 135200 | tf_op jit(solution)/shard_map/ppermute | solution.py:348
  30.8 0.5 collective-permute-start.10
  31.3 2.0 %collective-permute-start.14 = (f32[1,256,128]{2,1,0:T(8,128)S(1)}, f32[1,256,128]{2,1,0:T(8,128)S(1)}, u32[]{:S(2)}, u32[]{:S(2)}) collective-permute-start(f32[1,256,128]{2,1,0:T(8,128)S(1)} %get-tuple-element.27.refs_0_), channel_id=1, source_target_pairs={{0,4},{4,0},{8,12},{12,8},{16,20},{20,16},{24,28},{28,24},{1,5},{5... | collective-permute-start | bytes 393224 | tf_op jit(solution)/shard_map/ppermute | solution.py:348
  33.3 1.8 %collective-permute-start.15 = (f32[1,256,128]{2,1,0:T(8,128)S(1)}, f32[1,256,128]{2,1,0:T(8,128)S(1)}, u32[]{:S(2)}, u32[]{:S(2)}) collective-permute-start(f32[1,256,128]{2,1,0:T(8,128)S(1)} %get-tuple-element.27.refs_0_), channel_id=1, source_target_pairs={{0,8},{4,12},{8,0},{12,4},{16,24},{20,28},{24,16},{28,20},{1,9},{5... | collective-permute-start | bytes 393224 | tf_op jit(solution)/shard_map/ppermute | solution.py:348
  35.5 2.7 %collective-permute-done.10.refs_0_ = f32[1,256,128]{2,1,0:T(8,128)S(1)} collective-permute-done((f32[1,256,128]{2,1,0:T(8,128)S(1)}, f32[1,256,128]{2,1,0:T(8,128)S(1)}, u32[]{:S(2)}, u32[]{:S(2)}) %collective-permute-start.10) | collective-permute-done | bytes 131104 | tf_op jit(solution)/shard_map/ppermute | solution.py:348
  38.1 1.5 %collective-permute-start.13 = (f32[1,256,128]{2,1,0:T(8,128)S(1)}, f32[1,256,128]{2,1,0:T(8,128)S(1)}, u32[]{:S(2)}, u32[]{:S(2)}) collective-permute-start(f32[1,256,128]{2,1,0:T(8,128)S(1)} %collective-permute-done.10.refs_0_), channel_id=1, source_target_pairs={{0,12},{4,8},{8,4},{12,0},{16,28},{20,24},{24,20},{28,16},{1,13},{... | collective-permute-start | bytes 393224 | tf_op jit(solution)/shard_map/ppermute | solution.py:348
  39.6 0.5 collective-permute-start.12
  40.2 1.5 %collective-permute-start.11 = (f32[1,256,128]{2,1,0:T(8,128)S(1)}, f32[1,256,128]{2,1,0:T(8,128)S(1)}, u32[]{:S(2)}, u32[]{:S(2)}) collective-permute-start(f32[1,256,128]{2,1,0:T(8,128)S(1)} %collective-permute-done.10.refs_0_), channel_id=1, source_target_pairs={{0,8},{4,12},{8,0},{12,4},{16,24},{20,28},{24,16},{28,20},{1,9},{5... | collective-permute-start | bytes 393224 | tf_op jit(solution)/shard_map/ppermute | solution.py:348
  41.6 2.4 %collective-permute-done.16.refs_3_ = f32[1,256,128]{2,1,0:T(8,128)S(1)} collective-permute-done((f32[1,256,128]{2,1,0:T(8,128)S(1)}, f32[1,256,128]{2,1,0:T(8,128)S(1)}, u32[]{:S(2)}, u32[]{:S(2)}) %collective-permute-start.16) | collective-permute-done | bytes 131104 | tf_op jit(solution)/shard_map/ppermute | solution.py:348
  44.0 0.7 %backward.3.refs_3_ = f32[272,512]{1,0:T(8,128)S(1)} custom-call(f32[1,256,128]{2,1,0:T(8,128)S(1)} %get-tuple-element.27.refs_0_, f32[1,256,128]{2,1,0:T(8,128)S(1)} %collective-permute-done.14.refs_1_, f32[1,256,128]{2,1,0:T(8,128)S(1)} %collective-permute-done.15.refs_2_, f32[1,256,128]{2,1,0:T(8,128)S(1)} %collective-permute-done.16.refs_3_, ...), custom_call_target="tpu_custom_call" | custom-call | flops 536870912 | bytes 2097152 | tf_op jit(solution)/shard_map/backward/pallas_call | solution.py:265
  44.8 0.8 %collective-permute-done.13.refs_1_ = f32[1,256,128]{2,1,0:T(8,128)S(1)} collective-permute-done((f32[1,256,128]{2,1,0:T(8,128)S(1)}, f32[1,256,128]{2,1,0:T(8,128)S(1)}, u32[]{:S(2)}, u32[]{:S(2)}) %collective-permute-start.13) | collective-permute-done | bytes 131104 | tf_op jit(solution)/shard_map/ppermute | solution.py:348
  45.5 0.5 backward.4.refs_2_
  46.0 0.5 collective-permute-done.12.refs_0_
  47.4 1.1 %collective-permute-done.17 = f32[2,136,128]{2,1,0:T(8,128)S(1)} collective-permute-done((f32[2,136,128]{2,1,0:T(8,128)S(1)}, f32[2,136,128]{2,1,0:T(8,128)S(1)}, u32[]{:S(2)}, u32[]{:S(2)}) %collective-permute-start.17) | collective-permute-done | bytes 139296 | tf_op jit(solution)/shard_map/ppermute | solution.py:348
  48.5 1.4 %collective-permute-start.18 = (f32[1,136,128]{2,1,0:T(8,128)S(1)}, f32[1,136,128]{2,1,0:T(8,128)S(1)}, u32[]{:S(2)}, u32[]{:S(2)}) collective-permute-start(f32[1,136,128]{2,1,0:T(8,128)S(1)} %slice_add_fusion), channel_id=1, source_target_pairs={{0,2},{1,3},{2,0},{3,1},{4,6},{5,7},{6,4},{7,5},{8,10},{9,11},{10,... | collective-permute-start | bytes 208904 | tf_op jit(solution)/shard_map/ppermute | solution.py:348
  50.0 0.8 %shard_map.87 = f32[256,128]{1,0:T(8,128)} custom-call(f32[256,128]{1,0:T(8,128)S(1)} %get-tuple-element.26.resid_ref), custom_call_target="tpu_custom_call" | custom-call | flops 32768 | bytes 262144 | tf_op jit(solution)/shard_map/pallas_call | solution.py:336
  50.7 2.1 %collective-permute-done.18 = f32[1,136,128]{2,1,0:T(8,128)S(1)} collective-permute-done((f32[1,136,128]{2,1,0:T(8,128)S(1)}, f32[1,136,128]{2,1,0:T(8,128)S(1)}, u32[]{:S(2)}, u32[]{:S(2)}) %collective-permute-start.18) | collective-permute-done | bytes 69664 | tf_op jit(solution)/shard_map/ppermute | solution.py:348
  52.9 0.7 %copy.10 = f32[128,128]{1,0:T(8,128)} copy(f32[128,128]{0,1:T(8,128)S(1)} %fusion.4) | data formatting | bytes 131072
  (31 shorter events, 1.9 us)
Async XLA Ops:
  0.6 9.4 %copy-start = (f32[128,128]{1,0:T(8,128)S(1)}, f32[128,128]{1,0:T(8,128)}, u32[]{:S(2)}) copy-start(f32[128,128]{1,0:T(8,128)} %refs_0_.1) | copy-start | bytes 196612
  0.6 9.3 %collective-permute-start = (f32[128,128]{1,0:T(8,128)}, f32[128,128]{1,0:T(8,128)S(1)}, u32[]{:S(2)}, u32[]{:S(2)}) collective-permute-start(f32[128,128]{1,0:T(8,128)} %refs_0_.1), channel_id=1, source_target_pairs={{0,1},{1,0},{2,3},{3,2},{4,5},{5,4},{6,7},{7,6},{8,9},{9,8},{10,11... | collective-permute-start | bytes 196616 | tf_op jit(solution)/shard_map/ppermute | solution.py:348
  1.2 8.8 %collective-permute-start.1 = (f32[128,128]{1,0:T(8,128)}, f32[128,128]{1,0:T(8,128)S(1)}, u32[]{:S(2)}, u32[]{:S(2)}) collective-permute-start(f32[128,128]{1,0:T(8,128)} %refs_0_.1), channel_id=1, source_target_pairs={{0,2},{1,3},{2,0},{3,1},{4,6},{5,7},{6,4},{7,5},{8,10},{9,11},{10,... | collective-permute-start | bytes 196616 | tf_op jit(solution)/shard_map/ppermute | solution.py:348
  3.8 6.2 %collective-permute-start.2 = (f32[128,128]{1,0:T(8,128)}, f32[128,128]{1,0:T(8,128)S(1)}, u32[]{:S(2)}, u32[]{:S(2)}) collective-permute-start(f32[128,128]{1,0:T(8,128)} %refs_0_.1), channel_id=1, source_target_pairs={{0,3},{1,2},{2,1},{3,0},{4,7},{5,6},{6,5},{7,4},{8,11},{9,10},{10,... | collective-permute-start | bytes 196616 | tf_op jit(solution)/shard_map/ppermute | solution.py:348
  4.4 20.0 %copy-start.1 = (f32[1,256,128]{2,1,0:T(8,128)S(1)}, f32[1,256,128]{2,1,0:T(8,128)}, u32[]{:S(2)}) copy-start(f32[1,256,128]{2,1,0:T(8,128)} %param.13) | copy-start | bytes 393220
  10.7 7.9 %collective-permute-start.6 = (f32[1,264,128]{2,1,0:T(8,128)S(1)}, f32[1,264,128]{2,1,0:T(8,128)S(1)}, u32[]{:S(2)}, u32[]{:S(2)}) collective-permute-start(f32[1,264,128]{2,1,0:T(8,128)S(1)} %get-tuple-element.17), channel_id=1, source_target_pairs={{0,8},{4,12},{8,0},{12,4},{16,24},{20,28},{24,16},{28,20},{1,9},{5... | collective-permute-start | bytes 405512 | tf_op jit(solution)/shard_map/ppermute | solution.py:348
  12.6 9.2 %collective-permute-start.7 = (f32[1,264,128]{2,1,0:T(8,128)S(1)}, f32[1,264,128]{2,1,0:T(8,128)S(1)}, u32[]{:S(2)}, u32[]{:S(2)}) collective-permute-start(f32[1,264,128]{2,1,0:T(8,128)S(1)} %get-tuple-element.18), channel_id=1, source_target_pairs={{0,4},{4,0},{8,12},{12,8},{16,20},{20,16},{24,28},{28,24},{1,5},{5... | collective-permute-start | bytes 405512 | tf_op jit(solution)/shard_map/ppermute | solution.py:348
  14.1 7.7 %collective-permute-start.8 = (f32[1,264,128]{2,1,0:T(8,128)S(1)}, f32[1,264,128]{2,1,0:T(8,128)S(1)}, u32[]{:S(2)}, u32[]{:S(2)}) collective-permute-start(f32[1,264,128]{2,1,0:T(8,128)S(1)} %get-tuple-element.19), channel_id=1, source_target_pairs={{0,12},{4,8},{8,4},{12,0},{16,28},{20,24},{24,20},{28,16},{1,13},{... | collective-permute-start | bytes 405512 | tf_op jit(solution)/shard_map/ppermute | solution.py:348
  15.2 9.8 %collective-permute-start.3 = (f32[1,264,128]{2,1,0:T(8,128)S(1)}, f32[1,264,128]{2,1,0:T(8,128)S(1)}, u32[]{:S(2)}, u32[]{:S(2)}) collective-permute-start(f32[1,264,128]{2,1,0:T(8,128)S(1)} %get-tuple-element.13), channel_id=1, source_target_pairs={{0,4},{4,0},{8,12},{12,8},{16,20},{20,16},{24,28},{28,24},{1,5},{5... | collective-permute-start | bytes 405512 | tf_op jit(solution)/shard_map/ppermute | solution.py:348
  17.0 8.0 %collective-permute-start.4 = (f32[1,264,128]{2,1,0:T(8,128)S(1)}, f32[1,264,128]{2,1,0:T(8,128)S(1)}, u32[]{:S(2)}, u32[]{:S(2)}) collective-permute-start(f32[1,264,128]{2,1,0:T(8,128)S(1)} %get-tuple-element.14), channel_id=1, source_target_pairs={{0,8},{4,12},{8,0},{12,4},{16,24},{20,28},{24,16},{28,20},{1,9},{5... | collective-permute-start | bytes 405512 | tf_op jit(solution)/shard_map/ppermute | solution.py:348
  18.6 9.5 %collective-permute-start.5 = (f32[1,264,128]{2,1,0:T(8,128)S(1)}, f32[1,264,128]{2,1,0:T(8,128)S(1)}, u32[]{:S(2)}, u32[]{:S(2)}) collective-permute-start(f32[1,264,128]{2,1,0:T(8,128)S(1)} %get-tuple-element.15), channel_id=1, source_target_pairs={{0,12},{4,8},{8,4},{12,0},{16,28},{20,24},{24,20},{28,16},{1,13},{... | collective-permute-start | bytes 405512 | tf_op jit(solution)/shard_map/ppermute | solution.py:348
  21.8 8.9 %collective-permute-start.9 = (f32[1,264,128]{2,1,0:T(8,128)S(1)}, f32[1,264,128]{2,1,0:T(8,128)S(1)}, u32[]{:S(2)}, u32[]{:S(2)}) collective-permute-start(f32[1,264,128]{2,1,0:T(8,128)S(1)} %add_add_fusion), channel_id=1, source_target_pairs={{0,16},{4,20},{8,24},{12,28},{16,0},{20,4},{24,8},{28,12},{1,17},{... | collective-permute-start | bytes 405512 | tf_op jit(solution)/shard_map/ppermute | solution.py:348
  30.8 7.3 %collective-permute-start.10 = (f32[1,256,128]{2,1,0:T(8,128)S(1)}, f32[1,256,128]{2,1,0:T(8,128)S(1)}, u32[]{:S(2)}, u32[]{:S(2)}) collective-permute-start(f32[1,256,128]{2,1,0:T(8,128)S(1)} %get-tuple-element.27.refs_0_), channel_id=1, source_target_pairs={{0,16},{4,20},{8,24},{12,28},{16,0},{20,4},{24,8},{28,12},{1,17},{... | collective-permute-start | bytes 393224 | tf_op jit(solution)/shard_map/ppermute | solution.py:348
  31.3 8.9 %collective-permute-start.14 = (f32[1,256,128]{2,1,0:T(8,128)S(1)}, f32[1,256,128]{2,1,0:T(8,128)S(1)}, u32[]{:S(2)}, u32[]{:S(2)}) collective-permute-start(f32[1,256,128]{2,1,0:T(8,128)S(1)} %get-tuple-element.27.refs_0_), channel_id=1, source_target_pairs={{0,4},{4,0},{8,12},{12,8},{16,20},{20,16},{24,28},{28,24},{1,5},{5... | collective-permute-start | bytes 393224 | tf_op jit(solution)/shard_map/ppermute | solution.py:348
  33.3 8.3 %collective-permute-start.15 = (f32[1,256,128]{2,1,0:T(8,128)S(1)}, f32[1,256,128]{2,1,0:T(8,128)S(1)}, u32[]{:S(2)}, u32[]{:S(2)}) collective-permute-start(f32[1,256,128]{2,1,0:T(8,128)S(1)} %get-tuple-element.27.refs_0_), channel_id=1, source_target_pairs={{0,8},{4,12},{8,0},{12,4},{16,24},{20,28},{24,16},{28,20},{1,9},{5... | collective-permute-start | bytes 393224 | tf_op jit(solution)/shard_map/ppermute | solution.py:348
  35.1 9.0 %collective-permute-start.16 = (f32[1,256,128]{2,1,0:T(8,128)S(1)}, f32[1,256,128]{2,1,0:T(8,128)S(1)}, u32[]{:S(2)}, u32[]{:S(2)}) collective-permute-start(f32[1,256,128]{2,1,0:T(8,128)S(1)} %get-tuple-element.27.refs_0_), channel_id=1, source_target_pairs={{0,12},{4,8},{8,4},{12,0},{16,28},{20,24},{24,20},{28,16},{1,13},{... | collective-permute-start | bytes 393224 | tf_op jit(solution)/shard_map/ppermute | solution.py:348
  38.1 7.4 %collective-permute-start.13 = (f32[1,256,128]{2,1,0:T(8,128)S(1)}, f32[1,256,128]{2,1,0:T(8,128)S(1)}, u32[]{:S(2)}, u32[]{:S(2)}) collective-permute-start(f32[1,256,128]{2,1,0:T(8,128)S(1)} %collective-permute-done.10.refs_0_), channel_id=1, source_target_pairs={{0,12},{4,8},{8,4},{12,0},{16,28},{20,24},{24,20},{28,16},{1,13},{... | collective-permute-start | bytes 393224 | tf_op jit(solution)/shard_map/ppermute | solution.py:348
  39.6 6.8 %collective-permute-start.12 = (f32[1,256,128]{2,1,0:T(8,128)S(1)}, f32[1,256,128]{2,1,0:T(8,128)S(1)}, u32[]{:S(2)}, u32[]{:S(2)}) collective-permute-start(f32[1,256,128]{2,1,0:T(8,128)S(1)} %collective-permute-done.10.refs_0_), channel_id=1, source_target_pairs={{0,4},{4,0},{8,12},{12,8},{16,20},{20,16},{24,28},{28,24},{1,5},{5... | collective-permute-start | bytes 393224 | tf_op jit(solution)/shard_map/ppermute | solution.py:348
  40.2 6.6 %collective-permute-start.11 = (f32[1,256,128]{2,1,0:T(8,128)S(1)}, f32[1,256,128]{2,1,0:T(8,128)S(1)}, u32[]{:S(2)}, u32[]{:S(2)}) collective-permute-start(f32[1,256,128]{2,1,0:T(8,128)S(1)} %collective-permute-done.10.refs_0_), channel_id=1, source_target_pairs={{0,8},{4,12},{8,0},{12,4},{16,24},{20,28},{24,16},{28,20},{1,9},{5... | collective-permute-start | bytes 393224 | tf_op jit(solution)/shard_map/ppermute | solution.py:348
  47.0 1.4 %collective-permute-start.17 = (f32[2,136,128]{2,1,0:T(8,128)S(1)}, f32[2,136,128]{2,1,0:T(8,128)S(1)}, u32[]{:S(2)}, u32[]{:S(2)}) collective-permute-start(f32[2,136,128]{2,1,0:T(8,128)S(1)} %finish.3), channel_id=1, source_target_pairs={{0,1},{1,0},{2,3},{3,2},{4,5},{5,4},{6,7},{7,6},{8,9},{9,8},{10,11... | collective-permute-start | bytes 417800 | tf_op jit(solution)/shard_map/ppermute | solution.py:348
  48.5 4.4 %collective-permute-start.18 = (f32[1,136,128]{2,1,0:T(8,128)S(1)}, f32[1,136,128]{2,1,0:T(8,128)S(1)}, u32[]{:S(2)}, u32[]{:S(2)}) collective-permute-start(f32[1,136,128]{2,1,0:T(8,128)S(1)} %slice_add_fusion), channel_id=1, source_target_pairs={{0,2},{1,3},{2,0},{3,1},{4,6},{5,7},{6,4},{7,5},{8,10},{9,11},{10,... | collective-permute-start | bytes 208904 | tf_op jit(solution)/shard_map/ppermute | solution.py:348
